TPU v7x, 32 devices: a whole 2x2x4 slice. The times are simulated.
32 devices in a mesh: narrow: 4 (over z), wide: 8 (over y, x, core).
Axes of the slice: x: 2, y: 2, z: 4, core: 2. Of those that a mesh axis runs over, the one named last changes fastest.
Arguments:
- tokens: bfloat16 [12288, 640], P('wide'), may hold values from -6 to 6
- cotangent: bfloat16 [12288, 640], P('wide'), may hold values from -6 to 6
- seq_lens: int32 [8, 16], P('wide'), may hold values from 1 to 1024, 1536 in all within a row
- norm_gains: bfloat16 [2, 640], replicated, may hold values from 0.099609375 to 1.8984375
- norm_shifts: bfloat16 [2, 640], replicated, may hold values from -3 to 3
- w_qkv: bfloat16 [3, 640, 640], P(None, 'wide', 'narrow'), may hold values from -0.25 to 0.25
- w_attn_out: bfloat16 [640, 640], P('narrow', 'wide'), may hold values from -2 to 2
- w_ffn_in: bfloat16 [640, 5120], P('narrow', 'wide'), may hold values from -0.25 to 0.25
- w_ffn_down: bfloat16 [640, 5120], P('narrow', 'wide'), may hold values from -0.078125 to 0.078125
Outputs:
- layer_out: bfloat16 [12288, 640], P('wide')
- input_grad: bfloat16 [12288, 640], P('wide')
- grad_norm_gains: float32 [2, 640], P(None, 'wide')
- grad_norm_shifts: float32 [2, 640], P(None, 'wide')
- grad_qkv: float32 [3, 640, 640], P(None, 'wide', 'narrow')
- grad_attn_out: float32 [640, 640], P('narrow', 'wide')
- grad_ffn_in: float32 [640, 5120], P('narrow', 'wide')
- grad_ffn_down: float32 [640, 5120], P('narrow', 'wide')
Inputs may be any that keep to these rules, and one draw needn't show every extreme that they name: `seq_lens`: each row lists the lengths of the 16 sequences packed end to end in that index's 1536 slots; a row sums to 1536 and its largest entry is exactly 1024.
All inputs are finite; a program needn't handle non-finite values.
Results may differ from a plain program's by a relative error of at most 0.015.
Values may be sent and summed in bfloat16 or wider, within the bound.
No kernel may reach another device: no remote copies, remote signals or barrier semaphores. Data moves between devices by JAX's collectives and lax.ppermute only.
A program may use at most 128 MiB of HBM per device.

v0:
```python
from functools import partial
import jax
import jax.numpy as jnp
from jax import lax
from jax.sharding import PartitionSpec as P

HD = 32
QBLK = 512
FBLK = 128
EPS = 1e-05


def layer_norm(rows, gain, shift):
    center = rows - jnp.mean(rows, axis=-1, keepdims=True)
    spread = jnp.mean(center * center, axis=-1, keepdims=True)
    return center * lax.rsqrt(spread + EPS) * gain + shift


def segment_ids(lengths, count):
    ends = jnp.cumsum(lengths, dtype=jnp.int32)
    position = jnp.arange(count, dtype=jnp.int32)
    return jnp.sum((position[:, None] >= ends[None, :]).astype(jnp.int32), axis=1)


def block_scores(q_block, keys, seg_block, segment):
    scores = jnp.einsum("qd,kd->qk", q_block, keys, preferred_element_type=jnp.float32) * HD ** (
        -0.5
    )
    return jnp.where(seg_block[:, None] == segment[None, :], scores, -1e30)


def attend_forward(query, key, value, segment):
    count, width = query.shape
    starts = jnp.arange(count // QBLK, dtype=jnp.int32) * QBLK

    def one_head(head):
        q_head = lax.dynamic_slice_in_dim(query, head * HD, HD, 1)
        k_head = lax.dynamic_slice_in_dim(key, head * HD, HD, 1)
        v_head = lax.dynamic_slice_in_dim(value, head * HD, HD, 1)

        def one_block(start):
            q_block = lax.dynamic_slice_in_dim(q_head, start, QBLK, 0)
            seg_block = lax.dynamic_slice_in_dim(segment, start, QBLK, 0)
            scores = block_scores(q_block, k_head, seg_block, segment)
            top = jnp.max(scores, axis=1, keepdims=True)
            expd = jnp.exp(scores - top)
            total = jnp.sum(expd, axis=1, keepdims=True)
            weights = (expd / total).astype(jnp.bfloat16)
            result = jnp.dot(weights, v_head, preferred_element_type=jnp.float32)
            return (result, (top + jnp.log(total))[:, 0])

        results, logsum = lax.map(one_block, starts)
        return (results.reshape(count, HD), logsum.reshape(count))

    results, logsum = lax.map(one_head, jnp.arange(width // HD, dtype=jnp.int32))
    return (results.transpose(1, 0, 2).reshape(count, width), logsum)


def attend_backward(query, key, value, dattended, logsum, segment):
    count, width = query.shape
    starts = jnp.arange(count // QBLK, dtype=jnp.int32) * QBLK
    scale = HD ** (-0.5)

    def one_head(head):
        q_head = lax.dynamic_slice_in_dim(query, head * HD, HD, 1)
        k_head = lax.dynamic_slice_in_dim(key, head * HD, HD, 1)
        v_head = lax.dynamic_slice_in_dim(value, head * HD, HD, 1)
        d_head = lax.dynamic_slice_in_dim(dattended, head * HD, HD, 1)
        log_head = logsum[head]

        def one_block(carry, start):
            dkey, dvalue = carry
            q_block = lax.dynamic_slice_in_dim(q_head, start, QBLK, 0)
            d_block = lax.dynamic_slice_in_dim(d_head, start, QBLK, 0)
            seg_block = lax.dynamic_slice_in_dim(segment, start, QBLK, 0)
            log_block = lax.dynamic_slice_in_dim(log_head, start, QBLK, 0)
            scores = block_scores(q_block, k_head, seg_block, segment)
            prob = jnp.exp(scores - log_block[:, None])
            dprob = jnp.einsum("qd,kd->qk", d_block, v_head, preferred_element_type=jnp.float32)
            delta = jnp.sum(prob * dprob, axis=1, keepdims=True)
            dscore = (prob * (dprob - delta)).astype(jnp.bfloat16)
            dquery = jnp.dot(dscore, k_head, preferred_element_type=jnp.float32) * scale
            dkey = (
                dkey
                + jnp.einsum("qk,qd->kd", dscore, q_block, preferred_element_type=jnp.float32)
                * scale
            )
            dvalue = dvalue + jnp.einsum(
                "qk,qd->kd", prob.astype(jnp.bfloat16), d_block, preferred_element_type=jnp.float32
            )
            return ((dkey, dvalue), dquery)

        zeros = jnp.zeros((count, HD), jnp.float32)
        (dkey, dvalue), dquery = lax.scan(one_block, (zeros, zeros), starts)
        return (dquery.reshape(count, HD), dkey, dvalue)

    dquery, dkey, dvalue = lax.map(one_head, jnp.arange(width // HD, dtype=jnp.int32))

    def joined(arr):
        return arr.transpose(1, 0, 2).reshape(count, width)

    return (joined(dquery), joined(dkey), joined(dvalue))


def hidden_block(normed_mine, ffn_in_full, start):
    x_block = lax.dynamic_slice_in_dim(normed_mine, start, FBLK, 0)
    share = lax.psum_scatter(
        jnp.dot(x_block, ffn_in_full, preferred_element_type=jnp.float32),
        "narrow",
        scatter_dimension=0,
        tiled=True,
    )
    act_share = jax.nn.gelu(share, approximate=False).astype(jnp.bfloat16)
    act_rows = lax.all_gather(act_share, "narrow", axis=0, tiled=True)
    return (x_block, share, act_rows)


def local(
    tokens, cotangent, seq_lens, norm_gains, norm_shifts, w_qkv, w_attn_out, w_ffn_in, w_ffn_down
):
    count = tokens.shape[0]
    width = w_attn_out.shape[0]
    first_col = lax.axis_index("narrow") * width
    gains = norm_gains.astype(jnp.float32)
    shifts = norm_shifts.astype(jnp.float32)
    segment = segment_ids(seq_lens[0], count)
    resid = tokens.astype(jnp.float32)
    dy_full = cotangent.astype(jnp.float32)
    qkv_full, out_full = (
        lax.all_gather(w_qkv, "wide", axis=1, tiled=True),
        lax.all_gather(w_attn_out, "wide", axis=1, tiled=True),
    )
    normed_low = layer_norm(resid, gains[0], shifts[0]).astype(jnp.bfloat16)
    proj = jnp.einsum(
        "td,jde->jte", normed_low, qkv_full, preferred_element_type=jnp.float32
    ).astype(jnp.bfloat16)
    query, key, value = (proj[0], proj[1], proj[2])
    attended, logsum = attend_forward(query, key, value, segment)
    attended_low = attended.astype(jnp.bfloat16)
    mixed = jnp.dot(attended_low, out_full, preferred_element_type=jnp.float32)
    mixed_mine = lax.psum_scatter(mixed, "narrow", scatter_dimension=1, tiled=True)
    middle_mine = lax.dynamic_slice_in_dim(resid, first_col, width, 1) + mixed_mine
    middle = lax.all_gather(middle_mine, "narrow", axis=1, tiled=True)
    normed_two = layer_norm(middle, gains[1], shifts[1])
    ffn_in_part, ffn_down_part = (
        lax.all_gather(w_ffn_in, "wide", axis=1, tiled=True),
        lax.all_gather(w_ffn_down, "wide", axis=1, tiled=True),
    )
    dy_cols = lax.dynamic_slice_in_dim(cotangent, first_col, width, 1)
    normed_mine = lax.dynamic_slice_in_dim(normed_two, first_col, width, 1).astype(jnp.bfloat16)
    starts = jnp.arange(count // FBLK, dtype=jnp.int32) * FBLK

    def ffn_forward(carry, start):
        x_block, share, act_rows = hidden_block(normed_mine, ffn_in_part, start)
        result = lax.dot_general(
            act_rows, ffn_down_part, (((1,), (1,)), ((), ())), preferred_element_type=jnp.float32
        )
        return (carry, result)

    _, branch = lax.scan(ffn_forward, jnp.zeros((), jnp.float32), starts)
    branch_full = lax.all_gather(
        branch.reshape(count, width).astype(jnp.bfloat16), "narrow", axis=1, tiled=True
    ).astype(jnp.float32)
    layer_out = (middle + branch_full).astype(jnp.bfloat16)

    def ffn_backward(carry, start):
        grad_in, grad_down = carry
        x_block, share, act_rows = hidden_block(normed_mine, ffn_in_part, start)
        dy_block = lax.dynamic_slice_in_dim(dy_cols, start, FBLK, 0)
        dact = lax.psum_scatter(
            jnp.dot(dy_block, ffn_down_part, preferred_element_type=jnp.float32),
            "narrow",
            scatter_dimension=0,
            tiled=True,
        )
        _, gelu_back = jax.vjp(partial(jax.nn.gelu, approximate=False), share)
        dshare = gelu_back(dact)[0].astype(jnp.bfloat16)
        drows = lax.all_gather(dshare, "narrow", axis=0, tiled=True)
        grad_in = grad_in + lax.dot_general(
            x_block, drows, (((0,), (0,)), ((), ())), preferred_element_type=jnp.float32
        )
        grad_down = grad_down + lax.dot_general(
            dy_block, act_rows, (((0,), (0,)), ((), ())), preferred_element_type=jnp.float32
        )
        dnormed = lax.dot_general(
            drows, ffn_in_part, (((1,), (1,)), ((), ())), preferred_element_type=jnp.float32
        )
        return ((grad_in, grad_down), dnormed)

    empty = jnp.zeros(ffn_in_part.shape, jnp.float32)
    (grad_in, grad_down), dnormed = lax.scan(ffn_backward, (empty, empty), starts)
    dnormed_two = lax.all_gather(dnormed.reshape(count, width), "narrow", axis=1, tiled=True)
    grad_in_out, grad_down_out = (
        lax.psum_scatter(grad_in, "wide", scatter_dimension=1, tiled=True),
        lax.psum_scatter(grad_down, "wide", scatter_dimension=1, tiled=True),
    )
    _, norm_back_two = jax.vjp(layer_norm, middle, gains[1], shifts[1])
    dmiddle, dgain_two, dshift_two = norm_back_two(dnormed_two)
    dmiddle = dmiddle + dy_full
    dmixed_low = dmiddle.astype(jnp.bfloat16)
    grad_out = lax.dot_general(
        attended_low, dmixed_low, (((0,), (0,)), ((), ())), preferred_element_type=jnp.float32
    )
    dattended = lax.dot_general(
        dmixed_low, out_full, (((1,), (1,)), ((), ())), preferred_element_type=jnp.float32
    ).astype(jnp.bfloat16)
    dquery, dkey, dvalue = attend_backward(query, key, value, dattended, logsum, segment)
    dproj = jnp.stack([dquery, dkey, dvalue]).astype(jnp.bfloat16)
    grad_proj = jnp.einsum("td,jte->jde", normed_low, dproj, preferred_element_type=jnp.float32)
    dnormed_part = jnp.einsum("jte,jde->td", dproj, qkv_full, preferred_element_type=jnp.float32)
    dnormed_one = lax.psum(dnormed_part.astype(jnp.bfloat16), "narrow").astype(jnp.float32)
    _, norm_back_one = jax.vjp(layer_norm, resid, gains[0], shifts[0])
    dresid, dgain_one, dshift_one = norm_back_one(dnormed_one)
    input_grad = (dmiddle + dresid).astype(jnp.bfloat16)
    dgains = jnp.stack([dgain_one, dgain_two])
    dshifts = jnp.stack([dshift_one, dshift_two])
    gain_out, shift_out, proj_out, attn_out = (
        lax.psum_scatter(dgains, "wide", scatter_dimension=1, tiled=True),
        lax.psum_scatter(dshifts, "wide", scatter_dimension=1, tiled=True),
        lax.psum_scatter(grad_proj, "wide", scatter_dimension=1, tiled=True),
        lax.psum_scatter(grad_out, "wide", scatter_dimension=1, tiled=True),
    )
    return (
        layer_out,
        input_grad,
        gain_out,
        shift_out,
        proj_out,
        attn_out,
        grad_in_out,
        grad_down_out,
    )


def solution(mesh):
    placed = (
        P("wide", None),
        P("wide", None),
        P("wide", None),
        P(),
        P(),
        P(None, "wide", "narrow"),
        P("narrow", "wide"),
        P("narrow", "wide"),
        P("narrow", "wide"),
    )
    return jax.shard_map(
        local,
        mesh=mesh,
        in_specs=placed,
        out_specs=(
            P("wide", None),
            P("wide", None),
            P(None, "wide"),
            P(None, "wide"),
            P(None, "wide", "narrow"),
            P("narrow", "wide"),
            P("narrow", "wide"),
            P("narrow", "wide"),
        ),
        check_vma=False,
    )
```

profile of v0, /device:TPU:0, one launch (start us, length us, event | category | flops | bytes accessed | tf_op | source)
XLA Modules:
  0.0 4609.1 jit_solution(13928919483076880924)
XLA Ops:
  36.1 182.4 %while.84 = (s32[]{:T(128)}, bf16[5,1536,32]{1,2,0:T(8,128)(2,1)}, f32[5,1536]{1,0:T(8,128)}, s32[5]{0:T(128)}, bf16[1536,160]{1,0:T(8,128)(2,1)}, /*index=5*/bf...) while((s32[]{:T(128)}, bf16[5,1536,32]{1,2,0:T(8,128)(2,1)}, ...), condition=%wide.region_9.10_spmd.clone, body=%wide.region_4.9_spmd.clone.sunk | while | flops 107740680 | bytes 11363814 | solution.py:55
  236.6 69.2 %reduce-scatter.19.cloned.1.call-done = f32[1536,160]{0,1:T(8,128)} async-done(((f32[1536,640]{0,1:T(8,128)}), f32[1536,160]{0,1:T(8,128)}) %reduce-scatter.19.cloned.1.call-update) | async-done | bytes 983056 | tf_op jit(solution)/shard_map/reduce_scatter | solution.py:141
  312.1 73.2 %all-gather.9.cloned.1.call-done = f32[1536,640]{0,1:T(8,128)} async-done(((f32[1536,160]{0,1:T(8,128)}), f32[1536,640]{0,1:T(8,128)}) %all-gather.9.cloned.1.call-update) | async-done | bytes 3932176 | tf_op jit(solution)/shard_map/all_gather | solution.py:143
  439.6 2218.3 %while.87 = (s32[]{:T(128)}, f32[160,5120]{1,0:T(8,128)}, f32[160,5120]{1,0:T(8,128)}, f32[12,128,160]{1,0,2:T(8,128)}, s32[12]{0:T(128)S(1)}, /*index=5*/bf16[1...) while((s32[]{:T(128)}, f32[160,5120]{1,0:T(8,128)}, ...), condition=%wide.region_19.20_spmd.clone, body=%wide.region_16.19_spmd.clone.sunk | while | flops 1064796160 | bytes 83411448 | solution.py:191
  1239.3 50.9 %reduce-scatter.35.cloned.1.call-done = f32[32,5120]{1,0:T(8,128)} async-done(((f32[128,5120]{1,0:T(8,128)}), f32[32,5120]{1,0:T(8,128)}) %reduce-scatter.35.cloned.1.call-update) | async-done | bytes 655376 | tf_op jit(solution)/shard_map/while/body/eval_jaxpr/reduce_scatter | solution.py:170
  1794.0 50.9 %reduce-scatter.35.cloned.1.call-done = f32[32,5120]{1,0:T(8,128)} async-done(((f32[128,5120]{1,0:T(8,128)}), f32[32,5120]{1,0:T(8,128)}) %reduce-scatter.35.cloned.1.call-update) | async-done | bytes 655376 | tf_op jit(solution)/shard_map/while/body/eval_jaxpr/reduce_scatter | solution.py:170
  2163.8 50.9 %reduce-scatter.35.cloned.1.call-done = f32[32,5120]{1,0:T(8,128)} async-done(((f32[128,5120]{1,0:T(8,128)}), f32[32,5120]{1,0:T(8,128)}) %reduce-scatter.35.cloned.1.call-update) | async-done | bytes 655376 | tf_op jit(solution)/shard_map/while/body/eval_jaxpr/reduce_scatter | solution.py:170
  2533.6 50.9 %reduce-scatter.35.cloned.1.call-done = f32[32,5120]{1,0:T(8,128)} async-done(((f32[128,5120]{1,0:T(8,128)}), f32[32,5120]{1,0:T(8,128)}) %reduce-scatter.35.cloned.1.call-update) | async-done | bytes 655376 | tf_op jit(solution)/shard_map/while/body/eval_jaxpr/reduce_scatter | solution.py:170
  2660.5 1148.4 %while.82 = (s32[]{:T(128)}, bf16[12,128,160]{1,2,0:T(8,128)(2,1)}, s32[12]{0:T(128)S(1)}, bf16[1536,160]{1,0:T(8,128)(2,1)}, bf16[160,5120]{1,0:T(8,128)(2,1)},...) while((s32[]{:T(128)}, bf16[12,128,160]{1,2,0:T(8,128)(2,1)}, s32[12]{0:T(128)S(1)}, ...), condition=%wide.region_15.16_spmd, body=%wide.region_13.15_spmd.sunk | while | flops 430080000 | bytes 29638920 | solution.py:160
  2666.7 51.2 %reduce-scatter.33.cloned.1.call-done = f32[32,5120]{1,0:T(8,128)} async-done(((f32[128,5120]{1,0:T(8,128)}), f32[32,5120]{1,0:T(8,128)}) %reduce-scatter.33.cloned.1.call-update) | async-done | bytes 655376 | tf_op jit(solution)/shard_map/while/body/eval_jaxpr/reduce_scatter | solution.py:107
  2762.4 51.2 %reduce-scatter.33.cloned.1.call-done = f32[32,5120]{1,0:T(8,128)} async-done(((f32[128,5120]{1,0:T(8,128)}), f32[32,5120]{1,0:T(8,128)}) %reduce-scatter.33.cloned.1.call-update) | async-done | bytes 655376 | tf_op jit(solution)/shard_map/while/body/eval_jaxpr/reduce_scatter | solution.py:107
  2858.2 51.2 %reduce-scatter.33.cloned.1.call-done = f32[32,5120]{1,0:T(8,128)} async-done(((f32[128,5120]{1,0:T(8,128)}), f32[32,5120]{1,0:T(8,128)}) %reduce-scatter.33.cloned.1.call-update) | async-done | bytes 655376 | tf_op jit(solution)/shard_map/while/body/eval_jaxpr/reduce_scatter | solution.py:107
  2953.9 51.2 %reduce-scatter.33.cloned.1.call-done = f32[32,5120]{1,0:T(8,128)} async-done(((f32[128,5120]{1,0:T(8,128)}), f32[32,5120]{1,0:T(8,128)}) %reduce-scatter.33.cloned.1.call-update) | async-done | bytes 655376 | tf_op jit(solution)/shard_map/while/body/eval_jaxpr/reduce_scatter | solution.py:107
  3049.6 51.2 %reduce-scatter.33.cloned.1.call-done = f32[32,5120]{1,0:T(8,128)} async-done(((f32[128,5120]{1,0:T(8,128)}), f32[32,5120]{1,0:T(8,128)}) %reduce-scatter.33.cloned.1.call-update) | async-done | bytes 655376 | tf_op jit(solution)/shard_map/while/body/eval_jaxpr/reduce_scatter | solution.py:107
  3145.3 51.2 %reduce-scatter.33.cloned.1.call-done = f32[32,5120]{1,0:T(8,128)} async-done(((f32[128,5120]{1,0:T(8,128)}), f32[32,5120]{1,0:T(8,128)}) %reduce-scatter.33.cloned.1.call-update) | async-done | bytes 655376 | tf_op jit(solution)/shard_map/while/body/eval_jaxpr/reduce_scatter | solution.py:107
  3241.0 51.2 %reduce-scatter.33.cloned.1.call-done = f32[32,5120]{1,0:T(8,128)} async-done(((f32[128,5120]{1,0:T(8,128)}), f32[32,5120]{1,0:T(8,128)}) %reduce-scatter.33.cloned.1.call-update) | async-done | bytes 655376 | tf_op jit(solution)/shard_map/while/body/eval_jaxpr/reduce_scatter | solution.py:107
  3336.7 51.2 %reduce-scatter.33.cloned.1.call-done = f32[32,5120]{1,0:T(8,128)} async-done(((f32[128,5120]{1,0:T(8,128)}), f32[32,5120]{1,0:T(8,128)}) %reduce-scatter.33.cloned.1.call-update) | async-done | bytes 655376 | tf_op jit(solution)/shard_map/while/body/eval_jaxpr/reduce_scatter | solution.py:107
  3432.4 51.2 %reduce-scatter.33.cloned.1.call-done = f32[32,5120]{1,0:T(8,128)} async-done(((f32[128,5120]{1,0:T(8,128)}), f32[32,5120]{1,0:T(8,128)}) %reduce-scatter.33.cloned.1.call-update) | async-done | bytes 655376 | tf_op jit(solution)/shard_map/while/body/eval_jaxpr/reduce_scatter | solution.py:107
  3528.1 51.2 %reduce-scatter.33.cloned.1.call-done = f32[32,5120]{1,0:T(8,128)} async-done(((f32[128,5120]{1,0:T(8,128)}), f32[32,5120]{1,0:T(8,128)}) %reduce-scatter.33.cloned.1.call-update) | async-done | bytes 655376 | tf_op jit(solution)/shard_map/while/body/eval_jaxpr/reduce_scatter | solution.py:107
  3623.8 51.2 %reduce-scatter.33.cloned.1.call-done = f32[32,5120]{1,0:T(8,128)} async-done(((f32[128,5120]{1,0:T(8,128)}), f32[32,5120]{1,0:T(8,128)}) %reduce-scatter.33.cloned.1.call-update) | async-done | bytes 655376 | tf_op jit(solution)/shard_map/while/body/eval_jaxpr/reduce_scatter | solution.py:107
  3719.5 51.2 %reduce-scatter.33.cloned.1.call-done = f32[32,5120]{1,0:T(8,128)} async-done(((f32[128,5120]{1,0:T(8,128)}), f32[32,5120]{1,0:T(8,128)}) %reduce-scatter.33.cloned.1.call-update) | async-done | bytes 655376 | tf_op jit(solution)/shard_map/while/body/eval_jaxpr/reduce_scatter | solution.py:107
  3814.6 72.3 %all-gather.17.cloned.1.call-done = f32[1536,640]{0,1:T(8,128)} async-done(((f32[1536,160]{0,1:T(8,128)}), f32[1536,640]{0,1:T(8,128)}) %all-gather.17.cloned.1.call-update) | async-done | bytes 3932176 | tf_op jit(solution)/shard_map/all_gather | solution.py:192
  3942.7 319.0 %while.86 = (s32[]{:T(128)}, bf16[5,1536,32]{2,1,0:T(8,128)(2,1)}, bf16[5,1536,32]{1,2,0:T(8,128)(2,1)}, bf16[5,1536,32]{1,2,0:T(8,128)(2,1)}, s32[5]{0:T(128)},...) while((s32[]{:T(128)}, bf16[5,1536,32]{2,1,0:T(8,128)(2,1)}, ...), condition=%wide.region_26.27_spmd.clone, body=%wide.region_22.26_spmd.clone.sunk | while | flops 259784208 | bytes 27660404 | solution.py:97
  4281.8 67.5 %all-reduce.2.cloned.1.call-done = bf16[1536,640]{0,1:T(8,128)(2,1)} async-done(((bf16[1536,640]{0,1:T(8,128)(2,1)}), bf16[1536,640]{0,1:T(8,128)(2,1)}) %all-reduce.2.cloned.1.call-update) | async-done | bytes 1966096 | tf_op jit(solution)/shard_map/psum | solution.py:211
  (1048 shorter events, 3746.6 us)
Async XLA Ops:
  7.2 298.6 %reduce-scatter.19.cloned.1.call-start = ((), (), s32[]{:S(2)}) async-start(), calls=%async_computation.10 | async-start | bytes 4915200 | tf_op jit(solution)/shard_map/reduce_scatter | solution.py:141
  232.6 152.7 %all-gather.9.cloned.1.call-start = ((), (), s32[]{:S(2)}) async-start(), calls=%async_computation.11 | async-start | bytes 4915200 | tf_op jit(solution)/shard_map/all_gather | solution.py:143
  309.1 130.5 %all-gather.13.cloned.1.call-start = ((), (), s32[]{:S(2)}) async-start(), calls=%async_computation.13 | async-start | bytes 1843200 | tf_op jit(solution)/shard_map/all_gather | solution.py:147
  445.8 106.3 %reduce-scatter.35.cloned.1.call-start = ((), (), s32[]{:S(2)}) async-start(), calls=%async_computation.25 | async-start | bytes 3276800 | tf_op jit(solution)/shard_map/while/body/eval_jaxpr/reduce_scatter | solution.py:170
  447.9 139.0 %all-gather.21.cloned.1.call-start = ((), (), s32[]{:S(2)}) async-start(), calls=%async_computation.27 | async-start | bytes 1638400 | tf_op jit(solution)/shard_map/while/body/eval_jaxpr/all_gather | solution.py:178
  632.8 138.0 %all-gather.21.cloned.1.call-start = ((), (), s32[]{:S(2)}) async-start(), calls=%async_computation.27 | async-start | bytes 1638400 | tf_op jit(solution)/shard_map/while/body/eval_jaxpr/all_gather | solution.py:178
  817.5 138.0 %all-gather.21.cloned.1.call-start = ((), (), s32[]{:S(2)}) async-start(), calls=%async_computation.27 | async-start | bytes 1638400 | tf_op jit(solution)/shard_map/while/body/eval_jaxpr/all_gather | solution.py:178
  1002.3 138.0 %all-gather.21.cloned.1.call-start = ((), (), s32[]{:S(2)}) async-start(), calls=%async_computation.27 | async-start | bytes 1638400 | tf_op jit(solution)/shard_map/while/body/eval_jaxpr/all_gather | solution.py:178
  1187.0 138.1 %all-gather.21.cloned.1.call-start = ((), (), s32[]{:S(2)}) async-start(), calls=%async_computation.27 | async-start | bytes 1638400 | tf_op jit(solution)/shard_map/while/body/eval_jaxpr/all_gather | solution.py:178
  1371.9 138.0 %all-gather.21.cloned.1.call-start = ((), (), s32[]{:S(2)}) async-start(), calls=%async_computation.27 | async-start | bytes 1638400 | tf_op jit(solution)/shard_map/while/body/eval_jaxpr/all_gather | solution.py:178
  1556.7 138.0 %all-gather.21.cloned.1.call-start = ((), (), s32[]{:S(2)}) async-start(), calls=%async_computation.27 | async-start | bytes 1638400 | tf_op jit(solution)/shard_map/while/body/eval_jaxpr/all_gather | solution.py:178
  1741.6 138.1 %all-gather.21.cloned.1.call-start = ((), (), s32[]{:S(2)}) async-start(), calls=%async_computation.27 | async-start | bytes 1638400 | tf_op jit(solution)/shard_map/while/body/eval_jaxpr/all_gather | solution.py:178
  1926.5 138.1 %all-gather.21.cloned.1.call-start = ((), (), s32[]{:S(2)}) async-start(), calls=%async_computation.27 | async-start | bytes 1638400 | tf_op jit(solution)/shard_map/while/body/eval_jaxpr/all_gather | solution.py:178
  2111.5 138.1 %all-gather.21.cloned.1.call-start = ((), (), s32[]{:S(2)}) async-start(), calls=%async_computation.27 | async-start | bytes 1638400 | tf_op jit(solution)/shard_map/while/body/eval_jaxpr/all_gather | solution.py:178
  2296.5 138.0 %all-gather.21.cloned.1.call-start = ((), (), s32[]{:S(2)}) async-start(), calls=%async_computation.27 | async-start | bytes 1638400 | tf_op jit(solution)/shard_map/while/body/eval_jaxpr/all_gather | solution.py:178
  2481.2 138.1 %all-gather.21.cloned.1.call-start = ((), (), s32[]{:S(2)}) async-start(), calls=%async_computation.27 | async-start | bytes 1638400 | tf_op jit(solution)/shard_map/while/body/eval_jaxpr/all_gather | solution.py:178
  3809.7 120.9 %all-gather.15.cloned.1.call-start = ((), (), s32[]{:S(2)}) async-start(), calls=%async_computation.14 | async-start | bytes 2457600 | tf_op jit(solution)/shard_map/all_gather | solution.py:161
  3811.6 537.6 %all-reduce.2.cloned.1.call-start = ((), (), s32[]{:S(2)}) async-start(), calls=%async_computation.16 | async-start | bytes 3932160 | tf_op jit(solution)/shard_map/psum | solution.py:211
  4268.3 117.7 %reduce-scatter.31.cloned.1.call-start = ((), (), s32[]{:S(2)}) async-start(), calls=%async_computation.22 | async-start | bytes 737280
  4271.6 155.6 %reduce-scatter.29.cloned.1.call-start = ((), (), s32[]{:S(2)}) async-start(), calls=%async_computation.21 | async-start | bytes 1474560
  4281.7 182.2 %reduce-scatter.27.cloned.1.call-start = ((), (), s32[]{:S(2)}) async-start(), calls=%async_computation.20 | async-start | bytes 368640
  4356.3 144.4 %reduce-scatter.25.cloned.1.call-start = ((), (), s32[]{:S(2)}) async-start(), calls=%async_computation.19 | async-start | bytes 368640
  4357.3 194.1 %reduce-scatter.21.cloned.1.call-start = ((), (), s32[]{:S(2)}) async-start(), calls=%async_computation.17 | async-start | bytes 3686400 | tf_op jit(solution)/shard_map/reduce_scatter | solution.py:194
  4357.9 244.4 %reduce-scatter.23.cloned.1.call-start = ((), (), s32[]{:S(2)}) async-start(), calls=%async_computation.18 | async-start | bytes 3686400 | tf_op jit(solution)/shard_map/reduce_scatter | solution.py:195
  (163 other events, 8291.0 us)
Sparse Core Ops, SparseCore 0:
  232.7 72.9 reduce-scatter.18
  308.5 76.8 all-gather.8
  445.9 52.0 reduce-scatter.36
  500.2 51.7 reduce-scatter.34
  684.1 51.7 reduce-scatter.34
  815.5 51.0 reduce-scatter.36
  868.8 51.7 reduce-scatter.34
  1000.3 51.0 reduce-scatter.36
  1053.6 51.7 reduce-scatter.34
  1238.4 51.7 reduce-scatter.34
  1369.9 51.0 reduce-scatter.36
  1423.2 51.7 reduce-scatter.34
  1608.0 51.7 reduce-scatter.34
  1739.6 51.0 reduce-scatter.36
  1793.1 51.7 reduce-scatter.34
  1977.9 51.7 reduce-scatter.34
  2162.9 51.7 reduce-scatter.34
  2294.5 51.1 reduce-scatter.36
  2347.8 51.7 reduce-scatter.34
  2532.7 51.7 reduce-scatter.34
  2666.8 51.1 reduce-scatter.32
  3336.7 51.0 reduce-scatter.32
  3811.4 75.4 all-gather.16
  4268.5 80.7 all-reduce.1
  (61 shorter events, 2296.3 us)
where the time goes:
time: 4630 us; the launch traced here: 4610 us
  waiting for transfers between devices  3470 us (75%)
  matrix products  501 us (11%)
  local copies, waits for them, and re-layouts  284 us (6%)
  other arithmetic  192 us (4%)
  loops' own time  119 us (3%)
    reduce_scatter x24, waiting for transfers between devices, hidden_block(): lax.psum_scatter(jnp.dot(x_block, ffn_in_full, preferred_element_type=jnp...  1200 us
    all_gather x24, waiting for transfers between devices, hidden_block(): act_rows = lax.all_gather(act_share, 'narrow', axis=0, tiled=True)  675 us
    reduce_scatter x12, waiting for transfers between devices, ffn_backward(): lax.psum_scatter(jnp.dot(dy_block, ffn_down_part, preferred_element_type=...  610 us
    all_gather x12, waiting for transfers between devices, ffn_backward(): drows = lax.all_gather(dshare, 'narrow', axis=0, tiled=True)  382 us
    unnamed x17, waiting for transfers between devices  126 us
  transfers between devices with their start and end apart: 85, of which 85 were waited for; matrix products, arithmetic and copies ran while one was open for 5% of the time, Pallas kernels for 0%

commit v1 on v0

--- a/solution.py
+++ b/solution.py
@@ -8,6 +8,29 @@
 QBLK = 512
 FBLK = 128
 EPS = 1e-05
+
+
+def in_order(blocks, dim):
+    blocks = jnp.moveaxis(blocks, 0, dim)
+    dims = blocks.shape
+    return blocks.reshape(*dims[:dim], dims[dim] * dims[dim + 1], *dims[dim + 2 :])
+
+
+def doubled(shard, axis):
+    devices, index = (lax.axis_size(axis), lax.axis_index(axis))
+    tiles, apart = (shard[None], 1)
+    while apart < devices:
+        partner_block = lax.ppermute(tiles, axis, [(i, i ^ apart) for i in range(devices)])
+        low = index & apart == 0
+        tiles = jnp.concatenate(
+            [jnp.where(low, tiles, partner_block), jnp.where(low, partner_block, tiles)]
+        )
+        apart *= 2
+    return tiles
+
+
+def doubled_up(x, axis, dim):
+    return in_order(doubled(x, axis), dim)
 
 
 def layer_norm(rows, gain, shift):
@@ -111,7 +134,7 @@
         tiled=True,
     )
     act_share = jax.nn.gelu(share, approximate=False).astype(jnp.bfloat16)
-    act_rows = lax.all_gather(act_share, "narrow", axis=0, tiled=True)
+    act_rows = doubled_up(act_share, "narrow", 0)
     return (x_block, share, act_rows)
 
 

time: 4630 us -> 4730 us (1.022)
    all_gather x24 -> x0, waiting for transfers between devices: 675 us -> none  [hidden_block(): act_rows = lax.all_gather(act_share, 'narrow', axis=0, tiled=True)]
    ppermute x0 -> x48, waiting for transfers between devices: none -> 613 us  [doubled(): lax.ppermute(tiles, axis, [(i, i ^ apart) for i in range(devices)])]
    reduce_scatter x12, waiting for transfers between devices: 610 us -> 705 us  [ffn_backward(): lax.psum_scatter(jnp.dot(dy_block, ffn_down_part, preferred_element_type=...]
    convert_element_type x24 -> x0, other arithmetic: 76.8 us -> none  [hidden_block(): act_share = jax.nn.gelu(share, approximate=False).astype(jnp.bfloat16)]
    broadcast_in_dim x0 -> x24, other arithmetic: none -> 60.3 us  [doubled(): tiles, apart = (shard[None], 1)]
  transfers between devices with their start and end apart: 85 -> 109, of which waited for: 85 -> 99; matrix products, arithmetic and copies ran while one was open for 5% -> 4% of each run, Pallas kernels for 0% -> 0%
where the time goes in v1:
time: 4730 us; the launch traced here: 4710 us
  waiting for transfers between devices  3510 us (74%)
  matrix products  481 us (10%)
  local copies, waits for them, and re-layouts  283 us (6%)
  other arithmetic  223 us (5%)
  loops' own time  122 us (3%)
  starting transfers between devices  48.1 us (1%)
    reduce_scatter x24, waiting for transfers between devices, hidden_block(): lax.psum_scatter(jnp.dot(x_block, ffn_in_full, preferred_element_type=jnp...  1220 us
    reduce_scatter x12, waiting for transfers between devices, ffn_backward(): lax.psum_scatter(jnp.dot(dy_block, ffn_down_part, preferred_element_type=...  705 us
    ppermute x48, waiting for transfers between devices, doubled(): lax.ppermute(tiles, axis, [(i, i ^ apart) for i in range(devices)])  613 us
    all_gather x12, waiting for transfers between devices, ffn_backward(): drows = lax.all_gather(dshare, 'narrow', axis=0, tiled=True)  385 us
    unnamed x17, waiting for transfers between devices  126 us
  transfers between devices with their start and end apart: 109, of which 99 were waited for; matrix products, arithmetic and copies ran while one was open for 4% of the time, Pallas kernels for 0%

profile of v1, /device:TPU:0, one launch (start us, length us, event | category | flops | bytes accessed | tf_op | source)
XLA Modules:
  0.0 4710.4 jit_solution(15729508198978797958)
XLA Ops:
  36.1 184.5 %while.84 = (s32[]{:T(128)}, bf16[5,1536,32]{1,2,0:T(8,128)(2,1)}, f32[5,1536]{1,0:T(8,128)}, s32[5]{0:T(128)}, bf16[1536,160]{1,0:T(8,128)(2,1)}, /*index=5*/bf...) while((s32[]{:T(128)}, bf16[5,1536,32]{1,2,0:T(8,128)(2,1)}, ...), condition=%wide.region_9.10_spmd.clone, body=%wide.region_4.9_spmd.clone.sunk | while | flops 107740680 | bytes 11363814 | solution.py:78
  238.6 69.2 %reduce-scatter.19.cloned.1.call-done = f32[1536,160]{0,1:T(8,128)} async-done(((f32[1536,640]{0,1:T(8,128)}), f32[1536,160]{0,1:T(8,128)}) %reduce-scatter.19.cloned.1.call-update) | async-done | bytes 983056 | tf_op jit(solution)/shard_map/reduce_scatter | solution.py:164
  314.2 73.2 %all-gather.7.cloned.1.call-done = f32[1536,640]{0,1:T(8,128)} async-done(((f32[1536,160]{0,1:T(8,128)}), f32[1536,640]{0,1:T(8,128)}) %all-gather.7.cloned.1.call-update) | async-done | bytes 3932176 | tf_op jit(solution)/shard_map/all_gather | solution.py:166
  441.6 2196.1 %while.87 = (s32[]{:T(128)}, f32[160,5120]{1,0:T(8,128)}, f32[160,5120]{1,0:T(8,128)}, f32[12,128,160]{1,0,2:T(8,128)}, s32[12]{0:T(128)S(1)}, /*index=5*/bf16[1...) while((s32[]{:T(128)}, f32[160,5120]{1,0:T(8,128)}, ...), condition=%wide.region_19.20_spmd.clone, body=%wide.region_16.19_spmd.clone.sunk | while | flops 1067089920 | bytes 92914320 | solution.py:214
  518.5 58.7 %reduce-scatter.35.cloned.1.call-done = f32[32,5120]{1,0:T(8,128)} async-done(((f32[128,5120]{1,0:T(8,128)}), f32[32,5120]{1,0:T(8,128)}) %reduce-scatter.35.cloned.1.call-update) | async-done | bytes 655376 | tf_op jit(solution)/shard_map/while/body/eval_jaxpr/reduce_scatter | solution.py:193
  700.2 59.2 %reduce-scatter.35.cloned.1.call-done = f32[32,5120]{1,0:T(8,128)} async-done(((f32[128,5120]{1,0:T(8,128)}), f32[32,5120]{1,0:T(8,128)}) %reduce-scatter.35.cloned.1.call-update) | async-done | bytes 655376 | tf_op jit(solution)/shard_map/while/body/eval_jaxpr/reduce_scatter | solution.py:193
  883.5 58.6 %reduce-scatter.35.cloned.1.call-done = f32[32,5120]{1,0:T(8,128)} async-done(((f32[128,5120]{1,0:T(8,128)}), f32[32,5120]{1,0:T(8,128)}) %reduce-scatter.35.cloned.1.call-update) | async-done | bytes 655376 | tf_op jit(solution)/shard_map/while/body/eval_jaxpr/reduce_scatter | solution.py:193
  1066.4 58.6 %reduce-scatter.35.cloned.1.call-done = f32[32,5120]{1,0:T(8,128)} async-done(((f32[128,5120]{1,0:T(8,128)}), f32[32,5120]{1,0:T(8,128)}) %reduce-scatter.35.cloned.1.call-update) | async-done | bytes 655376 | tf_op jit(solution)/shard_map/while/body/eval_jaxpr/reduce_scatter | solution.py:193
  1249.4 58.6 %reduce-scatter.35.cloned.1.call-done = f32[32,5120]{1,0:T(8,128)} async-done(((f32[128,5120]{1,0:T(8,128)}), f32[32,5120]{1,0:T(8,128)}) %reduce-scatter.35.cloned.1.call-update) | async-done | bytes 655376 | tf_op jit(solution)/shard_map/while/body/eval_jaxpr/reduce_scatter | solution.py:193
  1432.1 59.2 %reduce-scatter.35.cloned.1.call-done = f32[32,5120]{1,0:T(8,128)} async-done(((f32[128,5120]{1,0:T(8,128)}), f32[32,5120]{1,0:T(8,128)}) %reduce-scatter.35.cloned.1.call-update) | async-done | bytes 655376 | tf_op jit(solution)/shard_map/while/body/eval_jaxpr/reduce_scatter | solution.py:193
  1615.4 58.7 %reduce-scatter.35.cloned.1.call-done = f32[32,5120]{1,0:T(8,128)} async-done(((f32[128,5120]{1,0:T(8,128)}), f32[32,5120]{1,0:T(8,128)}) %reduce-scatter.35.cloned.1.call-update) | async-done | bytes 655376 | tf_op jit(solution)/shard_map/while/body/eval_jaxpr/reduce_scatter | solution.py:193
  1798.4 58.6 %reduce-scatter.35.cloned.1.call-done = f32[32,5120]{1,0:T(8,128)} async-done(((f32[128,5120]{1,0:T(8,128)}), f32[32,5120]{1,0:T(8,128)}) %reduce-scatter.35.cloned.1.call-update) | async-done | bytes 655376 | tf_op jit(solution)/shard_map/while/body/eval_jaxpr/reduce_scatter | solution.py:193
  1981.3 58.6 %reduce-scatter.35.cloned.1.call-done = f32[32,5120]{1,0:T(8,128)} async-done(((f32[128,5120]{1,0:T(8,128)}), f32[32,5120]{1,0:T(8,128)}) %reduce-scatter.35.cloned.1.call-update) | async-done | bytes 655376 | tf_op jit(solution)/shard_map/while/body/eval_jaxpr/reduce_scatter | solution.py:193
  2164.2 58.6 %reduce-scatter.35.cloned.1.call-done = f32[32,5120]{1,0:T(8,128)} async-done(((f32[128,5120]{1,0:T(8,128)}), f32[32,5120]{1,0:T(8,128)}) %reduce-scatter.35.cloned.1.call-update) | async-done | bytes 655376 | tf_op jit(solution)/shard_map/while/body/eval_jaxpr/reduce_scatter | solution.py:193
  2347.2 58.6 %reduce-scatter.35.cloned.1.call-done = f32[32,5120]{1,0:T(8,128)} async-done(((f32[128,5120]{1,0:T(8,128)}), f32[32,5120]{1,0:T(8,128)}) %reduce-scatter.35.cloned.1.call-update) | async-done | bytes 655376 | tf_op jit(solution)/shard_map/while/body/eval_jaxpr/reduce_scatter | solution.py:193
  2530.1 58.6 %reduce-scatter.35.cloned.1.call-done = f32[32,5120]{1,0:T(8,128)} async-done(((f32[128,5120]{1,0:T(8,128)}), f32[32,5120]{1,0:T(8,128)}) %reduce-scatter.35.cloned.1.call-update) | async-done | bytes 655376 | tf_op jit(solution)/shard_map/while/body/eval_jaxpr/reduce_scatter | solution.py:193
  2640.4 1269.5 %while.82 = (s32[]{:T(128)}, bf16[12,128,160]{1,2,0:T(8,128)(2,1)}, s32[12]{0:T(128)S(1)}, bf16[1536,160]{1,0:T(8,128)(2,1)}, bf16[160,5120]{1,0:T(8,128)(2,1)},...) while((s32[]{:T(128)}, bf16[12,128,160]{1,2,0:T(8,128)(2,1)}, ...), condition=%wide.region_15.16_spmd, body=%wide.region_13.15_spmd.sunk | while | flops 443023360 | bytes 36848008 | solution.py:183
  3386.5 52.3 %reduce-scatter.33.cloned.1.call-done = f32[32,5120]{1,0:T(8,128)} async-done(((f32[128,5120]{1,0:T(8,128)}), f32[32,5120]{1,0:T(8,128)}) %reduce-scatter.33.cloned.1.call-update) | async-done | bytes 655376 | tf_op jit(solution)/shard_map/while/body/eval_jaxpr/reduce_scatter | solution.py:130
  3492.4 52.3 %reduce-scatter.33.cloned.1.call-done = f32[32,5120]{1,0:T(8,128)} async-done(((f32[128,5120]{1,0:T(8,128)}), f32[32,5120]{1,0:T(8,128)}) %reduce-scatter.33.cloned.1.call-update) | async-done | bytes 655376 | tf_op jit(solution)/shard_map/while/body/eval_jaxpr/reduce_scatter | solution.py:130
  3704.2 52.3 %reduce-scatter.33.cloned.1.call-done = f32[32,5120]{1,0:T(8,128)} async-done(((f32[128,5120]{1,0:T(8,128)}), f32[32,5120]{1,0:T(8,128)}) %reduce-scatter.33.cloned.1.call-update) | async-done | bytes 655376 | tf_op jit(solution)/shard_map/while/body/eval_jaxpr/reduce_scatter | solution.py:130
  3810.1 52.3 %reduce-scatter.33.cloned.1.call-done = f32[32,5120]{1,0:T(8,128)} async-done(((f32[128,5120]{1,0:T(8,128)}), f32[32,5120]{1,0:T(8,128)}) %reduce-scatter.33.cloned.1.call-update) | async-done | bytes 655376 | tf_op jit(solution)/shard_map/while/body/eval_jaxpr/reduce_scatter | solution.py:130
  3915.4 73.2 %all-gather.15.cloned.1.call-done = f32[1536,640]{0,1:T(8,128)} async-done(((f32[1536,160]{0,1:T(8,128)}), f32[1536,640]{0,1:T(8,128)}) %all-gather.15.cloned.1.call-update) | async-done | bytes 3932176 | tf_op jit(solution)/shard_map/all_gather | solution.py:215
  4044.4 318.3 %while.86 = (s32[]{:T(128)}, bf16[5,1536,32]{2,1,0:T(8,128)(2,1)}, bf16[5,1536,32]{1,2,0:T(8,128)(2,1)}, bf16[5,1536,32]{1,2,0:T(8,128)(2,1)}, s32[5]{0:T(128)},...) while((s32[]{:T(128)}, bf16[5,1536,32]{2,1,0:T(8,128)(2,1)}, ...), condition=%wide.region_26.27_spmd.clone, body=%wide.region_22.26_spmd.clone.sunk | while | flops 259784208 | bytes 27660404 | solution.py:120
  4382.7 67.5 %all-reduce.2.cloned.1.call-done = bf16[1536,640]{0,1:T(8,128)(2,1)} async-done(((bf16[1536,640]{0,1:T(8,128)(2,1)}), bf16[1536,640]{0,1:T(8,128)(2,1)}) %all-reduce.2.cloned.1.call-update) | async-done | bytes 1966096 | tf_op jit(solution)/shard_map/psum | solution.py:234
  (1192 shorter events, 3749.0 us)
Async XLA Ops:
  7.2 300.6 %reduce-scatter.19.cloned.1.call-start = ((), (), s32[]{:S(2)}) async-start(), calls=%async_computation.10 | async-start | bytes 4915200 | tf_op jit(solution)/shard_map/reduce_scatter | solution.py:164
  234.7 152.7 %all-gather.7.cloned.1.call-start = ((), (), s32[]{:S(2)}) async-start(), calls=%async_computation.11 | async-start | bytes 4915200 | tf_op jit(solution)/shard_map/all_gather | solution.py:166
  311.1 130.5 %all-gather.9.cloned.1.call-start = ((), (), s32[]{:S(2)}) async-start(), calls=%async_computation.12 | async-start | bytes 1843200 | tf_op jit(solution)/shard_map/all_gather | solution.py:169
  448.4 128.7 %reduce-scatter.35.cloned.1.call-start = ((), (), s32[]{:S(2)}) async-start(), calls=%async_computation.24 | async-start | bytes 3276800 | tf_op jit(solution)/shard_map/while/body/eval_jaxpr/reduce_scatter | solution.py:193
  450.6 165.4 %all-gather.17.cloned.1.call-start = ((), (), s32[]{:S(2)}) async-start(), calls=%async_computation.26 | async-start | bytes 1638400 | tf_op jit(solution)/shard_map/while/body/eval_jaxpr/all_gather | solution.py:201
  631.3 128.1 %reduce-scatter.35.cloned.1.call-start = ((), (), s32[]{:S(2)}) async-start(), calls=%async_computation.24 | async-start | bytes 3276800 | tf_op jit(solution)/shard_map/while/body/eval_jaxpr/reduce_scatter | solution.py:193
  633.4 164.6 %all-gather.17.cloned.1.call-start = ((), (), s32[]{:S(2)}) async-start(), calls=%async_computation.26 | async-start | bytes 1638400 | tf_op jit(solution)/shard_map/while/body/eval_jaxpr/all_gather | solution.py:201
  816.5 164.4 %all-gather.17.cloned.1.call-start = ((), (), s32[]{:S(2)}) async-start(), calls=%async_computation.26 | async-start | bytes 1638400 | tf_op jit(solution)/shard_map/while/body/eval_jaxpr/all_gather | solution.py:201
  999.5 164.4 %all-gather.17.cloned.1.call-start = ((), (), s32[]{:S(2)}) async-start(), calls=%async_computation.26 | async-start | bytes 1638400 | tf_op jit(solution)/shard_map/while/body/eval_jaxpr/all_gather | solution.py:201
  1182.4 164.4 %all-gather.17.cloned.1.call-start = ((), (), s32[]{:S(2)}) async-start(), calls=%async_computation.26 | async-start | bytes 1638400 | tf_op jit(solution)/shard_map/while/body/eval_jaxpr/all_gather | solution.py:201
  1363.3 128.1 %reduce-scatter.35.cloned.1.call-start = ((), (), s32[]{:S(2)}) async-start(), calls=%async_computation.24 | async-start | bytes 3276800 | tf_op jit(solution)/shard_map/while/body/eval_jaxpr/reduce_scatter | solution.py:193
  1365.4 164.6 %all-gather.17.cloned.1.call-start = ((), (), s32[]{:S(2)}) async-start(), calls=%async_computation.26 | async-start | bytes 1638400 | tf_op jit(solution)/shard_map/while/body/eval_jaxpr/all_gather | solution.py:201
  1548.5 164.4 %all-gather.17.cloned.1.call-start = ((), (), s32[]{:S(2)}) async-start(), calls=%async_computation.26 | async-start | bytes 1638400 | tf_op jit(solution)/shard_map/while/body/eval_jaxpr/all_gather | solution.py:201
  1731.4 164.4 %all-gather.17.cloned.1.call-start = ((), (), s32[]{:S(2)}) async-start(), calls=%async_computation.26 | async-start | bytes 1638400 | tf_op jit(solution)/shard_map/while/body/eval_jaxpr/all_gather | solution.py:201
  1914.4 164.4 %all-gather.17.cloned.1.call-start = ((), (), s32[]{:S(2)}) async-start(), calls=%async_computation.26 | async-start | bytes 1638400 | tf_op jit(solution)/shard_map/while/body/eval_jaxpr/all_gather | solution.py:201
  2097.3 164.4 %all-gather.17.cloned.1.call-start = ((), (), s32[]{:S(2)}) async-start(), calls=%async_computation.26 | async-start | bytes 1638400 | tf_op jit(solution)/shard_map/while/body/eval_jaxpr/all_gather | solution.py:201
  2280.3 164.4 %all-gather.17.cloned.1.call-start = ((), (), s32[]{:S(2)}) async-start(), calls=%async_computation.26 | async-start | bytes 1638400 | tf_op jit(solution)/shard_map/while/body/eval_jaxpr/all_gather | solution.py:201
  2463.2 164.4 %all-gather.17.cloned.1.call-start = ((), (), s32[]{:S(2)}) async-start(), calls=%async_computation.26 | async-start | bytes 1638400 | tf_op jit(solution)/shard_map/while/body/eval_jaxpr/all_gather | solution.py:201
  3912.4 537.8 %all-reduce.2.cloned.1.call-start = ((), (), s32[]{:S(2)}) async-start(), calls=%async_computation.16 | async-start | bytes 3932160 | tf_op jit(solution)/shard_map/psum | solution.py:234
  4372.5 155.6 %reduce-scatter.29.cloned.1.call-start = ((), (), s32[]{:S(2)}) async-start(), calls=%async_computation.21 | async-start | bytes 1474560
  4382.6 182.3 %reduce-scatter.27.cloned.1.call-start = ((), (), s32[]{:S(2)}) async-start(), calls=%async_computation.20 | async-start | bytes 368640
  4457.3 144.2 %reduce-scatter.25.cloned.1.call-start = ((), (), s32[]{:S(2)}) async-start(), calls=%async_computation.19 | async-start | bytes 368640
  4458.3 194.1 %reduce-scatter.21.cloned.1.call-start = ((), (), s32[]{:S(2)}) async-start(), calls=%async_computation.17 | async-start | bytes 3686400 | tf_op jit(solution)/shard_map/reduce_scatter | solution.py:217
  4459.1 244.2 %reduce-scatter.23.cloned.1.call-start = ((), (), s32[]{:S(2)}) async-start(), calls=%async_computation.18 | async-start | bytes 3686400 | tf_op jit(solution)/shard_map/reduce_scatter | solution.py:218
  (199 other events, 6790.0 us)
Sparse Core Ops, SparseCore 0:
  234.8 72.9 reduce-scatter.18
  310.5 76.8 all-gather.6
  502.9 74.2 reduce-scatter.34
  684.9 74.4 reduce-scatter.34
  867.8 74.1 reduce-scatter.34
  1050.8 74.1 reduce-scatter.34
  1233.7 74.2 reduce-scatter.34
  1416.8 74.4 reduce-scatter.34
  1599.8 74.2 reduce-scatter.34
  1782.7 74.2 reduce-scatter.34
  1965.7 74.1 reduce-scatter.34
  2148.6 74.1 reduce-scatter.34
  2331.6 74.2 reduce-scatter.34
  2514.5 74.1 reduce-scatter.34
  2751.4 52.1 reduce-scatter.32
  3174.9 52.1 reduce-scatter.32
  3280.8 52.1 reduce-scatter.32
  3386.6 52.1 reduce-scatter.32
  3492.5 52.1 reduce-scatter.32
  3598.4 52.1 reduce-scatter.32
  3704.3 52.1 reduce-scatter.32
  3810.2 52.1 reduce-scatter.32
  3912.0 76.4 all-gather.14
  4369.4 80.7 all-reduce.1
  (37 shorter events, 1582.9 us)
